TPU v7x, 32 devices: a whole 2x2x4 slice. The times are simulated.
32 devices in a mesh: frame: 8 (over z, core), tok: 4 (over y, x).
Axes of the slice: x: 2, y: 2, z: 4, core: 2. Of those that a mesh axis runs over, the one named last changes fastest.
Arguments:
- stream: bfloat16 [8, 1024, 1152], P('frame', 'tok'), may hold values from -20 to 20
- queries: bfloat16 [8, 1024, 1152], P('frame', 'tok'), may hold values from -200 to 200
- key_vectors: bfloat16 [8, 1024, 1152], P('frame', 'tok'), may hold values from -6 to 6
- value_vectors: bfloat16 [8, 1024, 1152], P('frame', 'tok'), may hold values from -6 to 6
- modulation: float32 [8, 4, 1152], P('frame'), may hold values from -4 to 4
- output_weight: bfloat16 [1152, 1152], replicated, may hold values from -0.1875 to 0.1875
- output_bias: float32 [1152], replicated, may hold values from -3 to 3
- router_weight: bfloat16 [1152, 8], replicated, may hold values from -0.1875 to 0.1875
- expand_weight: bfloat16 [8, 1152, 4608], P('frame', None, 'tok'), may hold values from -0.1875 to 0.1875
- expand_bias: float32 [8, 4608], P('frame', 'tok'), may hold values from -3 to 3
- reduce_weight: bfloat16 [8, 4608, 1152], P('frame', 'tok'), may hold values from -0.09375 to 0.09375
- reduce_bias: float32 [8, 1152], P('frame'), may hold values from -3 to 3
- counts: int32 [8, 8], P(None, 'frame'), may hold values from 1 to 96, 256 in all within a row
- picked_rows: int32 [8, 8, 96], P(None, 'frame'), may hold values from 0 to 1023, as said below
Outputs:
- layer_out: bfloat16 [8, 1024, 1152], P('frame', 'tok')
Inputs may be any that keep to these rules, and one draw needn't show every extreme that they name: counts[e, g] slots of block (e, g) are used; the counts of one expert sum to 256. The entries of one block picked_rows[e, g, :] are distinct positions among the 1024 tokens of frame g; slots at or beyond counts[e, g] are unused.
All inputs are finite; a program needn't handle non-finite values.
Results may differ from a plain program's by a relative error of at most 0.0055.
Values may be sent and summed in bfloat16 or wider, within the bound.
A program may use at most 64 MiB of HBM per device.

v0:
```python
import math
import jax
import jax.numpy as jnp
from jax import lax
from jax.sharding import PartitionSpec as P

H = 16
HD = 72


def layer_norm(values):
    mean_val = jnp.mean(values, axis=-1, keepdims=True)
    centred = values - mean_val
    variance = jnp.mean(centred * centred, axis=-1, keepdims=True)
    return centred * lax.rsqrt(variance + 1e-06)


def head_attention(operands):
    head_queries, head_keys, head_values = operands
    length = head_queries.shape[1]
    block_rows = min(512, length)
    score_scale = 1.0 / math.sqrt(HD)

    def one_block(first_row):
        query_block = lax.dynamic_slice_in_dim(head_queries, first_row, block_rows, 1)
        scores = (
            lax.dot_general(
                query_block, head_keys, (((0,), (0,)), ((), ())), preferred_element_type=jnp.float32
            )
            * score_scale
        )
        scores = scores - jnp.max(scores, axis=1, keepdims=True)
        exponent = jnp.exp(scores)
        weights = (exponent / jnp.sum(exponent, axis=1, keepdims=True)).astype(jnp.bfloat16)
        return lax.dot_general(
            head_values, weights, (((1,), (1,)), ((), ())), preferred_element_type=jnp.float32
        ).astype(jnp.bfloat16)

    starts = jnp.arange(length // block_rows, dtype=jnp.int32) * block_rows
    blocks = lax.map(one_block, starts)
    return blocks.transpose(1, 0, 2).reshape(head_queries.shape[0], length)


def attend_items(pieces):
    outputs = lax.map(head_attention, (pieces[0][0], pieces[1][0], pieces[2][0]))
    return outputs[None]


def per_device(
    stream,
    queries,
    key_vectors,
    value_vectors,
    modulation,
    output_weight,
    output_bias,
    router_weight,
    expand_weight,
    expand_bias,
    reduce_weight,
    reduce_bias,
    counts,
    picked_rows,
):
    tok_groups = lax.axis_size("tok")
    tok_local = stream.shape[1]
    model_width = stream.shape[2]
    heads_local = H // tok_groups

    def to_heads(tensor):
        return tensor[0].reshape(tok_local, tok_groups, heads_local, HD).transpose(1, 2, 3, 0)

    attended = attend_items(
        (
            lax.all_to_all(to_heads(queries), "tok", split_axis=0, concat_axis=3, tiled=True),
            lax.all_to_all(to_heads(key_vectors), "tok", split_axis=0, concat_axis=3, tiled=True),
            lax.all_to_all(to_heads(value_vectors), "tok", split_axis=0, concat_axis=3, tiled=True),
        )
    )
    returned = lax.all_to_all(attended, "tok", split_axis=3, concat_axis=0, tiled=True)
    attended_rows = returned.transpose(3, 0, 1, 2).reshape(tok_local, model_width)
    projected = (
        jnp.dot(attended_rows, output_weight, preferred_element_type=jnp.float32) + output_bias
    )
    shares = modulation[0]
    residual = (stream[0].astype(jnp.float32) + shares[0] * projected).astype(jnp.bfloat16)
    normed = (layer_norm(residual.astype(jnp.float32)) * (1.0 + shares[2]) + shares[1]).astype(
        jnp.bfloat16
    )
    gate_values = jax.nn.sigmoid(jnp.dot(normed, router_weight, preferred_element_type=jnp.float32))
    slot_count = picked_rows.shape[2]
    local_pos = picked_rows[:, 0, :] - lax.axis_index("tok") * tok_local
    in_use = jnp.arange(slot_count, dtype=jnp.int32)[None, :] < counts
    on_shard = in_use & (local_pos >= 0) & (local_pos < tok_local)
    safe_pos = jnp.clip(local_pos, 0, tok_local - 1)
    chosen = jnp.take(normed, safe_pos, axis=0)
    chosen = jnp.where(on_shard[:, :, None], chosen, jnp.zeros_like(chosen))
    moved = lax.all_to_all(chosen, "frame", split_axis=0, concat_axis=1, tiled=True)
    expert_rows = lax.psum(moved.astype(jnp.float32).astype(jnp.bfloat16), "tok")
    hidden = jax.nn.gelu(
        jnp.einsum("erd,edf->erf", expert_rows, expand_weight, preferred_element_type=jnp.float32)
        + expand_bias[:, None, :],
        approximate=True,
    ).astype(jnp.bfloat16)
    partial_out = jnp.einsum(
        "erf,efd->erd", hidden, reduce_weight, preferred_element_type=jnp.float32
    )
    column_count = model_width // tok_groups
    summed = lax.psum_scatter(
        partial_out.astype(jnp.bfloat16), "tok", scatter_dimension=2, tiled=True
    ).astype(jnp.float32)
    bias_part = lax.dynamic_slice_in_dim(
        reduce_bias, lax.axis_index("tok") * column_count, column_count, 1
    )
    expert_out = (summed + bias_part[:, None, :]).astype(jnp.bfloat16)
    returned_cols = lax.all_to_all(expert_out, "frame", split_axis=1, concat_axis=0, tiled=True)
    returned_rows = lax.all_gather(returned_cols, "tok", axis=2, tiled=True)
    mix_weight = jnp.take_along_axis(gate_values.T, safe_pos, axis=1)
    mix_weight = jnp.where(on_shard, mix_weight, jnp.zeros_like(mix_weight)).astype(jnp.bfloat16)
    targets = jnp.arange(tok_local, dtype=jnp.int32)
    matches = (safe_pos.reshape(-1)[None, :] == targets[:, None]) & on_shard.reshape(-1)[None, :]
    scatter_table = jnp.where(matches, mix_weight.reshape(-1)[None, :], jnp.zeros((), jnp.bfloat16))
    expert_mix = jnp.dot(
        scatter_table, returned_rows.reshape(-1, model_width), preferred_element_type=jnp.float32
    )
    layer_out = (residual.astype(jnp.float32) + shares[3] * expert_mix).astype(jnp.bfloat16)
    return layer_out[None]


def solution(mesh):
    return jax.shard_map(
        per_device,
        mesh=mesh,
        in_specs=(
            P("frame", "tok", None),
            P("frame", "tok", None),
            P("frame", "tok", None),
            P("frame", "tok", None),
            P("frame", None, None),
            P(),
            P(),
            P(),
            P("frame", None, "tok"),
            P("frame", "tok"),
            P("frame", "tok", None),
            P("frame", None),
            P(None, "frame"),
            P(None, "frame", None),
        ),
        out_specs=P("frame", "tok", None),
        check_vma=False,
    )
```

profile of v0, /device:TPU:0, one launch (start us, length us, event | category | flops | bytes accessed | tf_op | source)
XLA Modules:
  0.0 382.8 jit_solution(11425842389973880382)
XLA Ops:
  8.8 5.2 %all-to-all-start = ((bf16[4,4,72,256]{3,2,1,0:T(8,128)(2,1)}), bf16[4,4,72,256]{3,2,1,0:T(8,128)(2,1)S(1)}, u32[]{:S(2)}, u32[]{:S(2)}) async-start(bf16[4,4,72,256]{3,2,1,0:T(8,128)(2,1)} %bitcast.128), calls=%async_computation | async-start | bytes 1179648 | tf_op jit(solution)/shard_map/all_to_all | solution.py:75
  16.1 6.6 %all-to-all-done = bf16[4,4,72,256]{3,2,1,0:T(8,128)(2,1)S(1)} async-done(((bf16[4,4,72,256]{3,2,1,0:T(8,128)(2,1)}), bf16[4,4,72,256]{3,2,1,0:T(8,128)(2,1)S(1)}, u32[]{:S(2)}, u32[]{:S(2)}) %all-to-all-start) | async-done | bytes 589856 | tf_op jit(solution)/shard_map/all_to_all | solution.py:75
  22.7 4.3 %all-to-all-start.1 = ((bf16[4,4,72,256]{3,2,1,0:T(8,128)(2,1)}), bf16[4,4,72,256]{3,2,1,0:T(8,128)(2,1)}, u32[]{:S(2)}, u32[]{:S(2)}) async-start(bf16[4,4,72,256]{3,2,1,0:T(8,128)(2,1)} %bitcast.127), calls=%async_computation.1 | async-start | bytes 1179648 | tf_op jit(solution)/shard_map/all_to_all | solution.py:76
  29.2 5.9 %all-to-all-done.1 = bf16[4,4,72,256]{3,2,1,0:T(8,128)(2,1)} async-done(((bf16[4,4,72,256]{3,2,1,0:T(8,128)(2,1)}), bf16[4,4,72,256]{3,2,1,0:T(8,128)(2,1)}, u32[]{:S(2)}, u32[]{:S(2)}) %all-to-all-start.1) | async-done | bytes 589856 | tf_op jit(solution)/shard_map/all_to_all | solution.py:76
  35.1 4.2 %all-to-all-start.2 = ((bf16[4,4,72,256]{3,2,1,0:T(8,128)(2,1)}), bf16[4,4,72,256]{3,2,1,0:T(8,128)(2,1)}, u32[]{:S(2)}, u32[]{:S(2)}) async-start(bf16[4,4,72,256]{3,2,1,0:T(8,128)(2,1)} %bitcast.126), calls=%async_computation.2 | async-start | bytes 1179648 | tf_op jit(solution)/shard_map/all_to_all | solution.py:77
  40.8 2.4 squeeze.27
  49.6 45.9 %while.21 = (s32[]{:T(128)}, bf16[4,72,1024]{2,1,0:T(8,128)(2,1)}, bf16[4,72,1024]{2,1,0:T(8,128)(2,1)}, bf16[4,72,1024]{2,1,0:T(8,128)(2,1)}, bf16[4,72,1024]{2...) while((s32[]{:T(128)}, bf16[4,72,1024]{2,1,0:T(8,128)(2,1)}, ...), condition=%wide.region_5.6_spmd, body=%wide.region_0.5_spmd.sunk | while | flops 155749376 | bytes 8513900 | solution.py:45
  51.6 8.6 %while.22 = (s32[]{:T(128)}, bf16[2,72,512]{2,1,0:T(8,128)(2,1)S(1)}, s32[2]{0:T(128)S(1)}, bf16[72,1024]{1,0:T(8,128)(2,1)S(1)}, bf16[72,1024]{1,0:T(8,128)(2,1...) while((s32[]{:T(128)}, bf16[2,72,512]{2,1,0:T(8,128)(2,1)S(1)}, ...), condition=%wide.region_4.4_spmd, body=%wide.region_1.3_spmd.sunk | while | flops 155749376 | bytes 6744219 | solution.py:40
  63.1 8.6 %while.22 = (s32[]{:T(128)}, bf16[2,72,512]{2,1,0:T(8,128)(2,1)S(1)}, s32[2]{0:T(128)S(1)}, bf16[72,1024]{1,0:T(8,128)(2,1)S(1)}, bf16[72,1024]{1,0:T(8,128)(2,1...) while((s32[]{:T(128)}, bf16[2,72,512]{2,1,0:T(8,128)(2,1)S(1)}, ...), condition=%wide.region_4.4_spmd, body=%wide.region_1.3_spmd.sunk | while | flops 155749376 | bytes 6744219 | solution.py:40
  74.6 8.6 %while.22 = (s32[]{:T(128)}, bf16[2,72,512]{2,1,0:T(8,128)(2,1)S(1)}, s32[2]{0:T(128)S(1)}, bf16[72,1024]{1,0:T(8,128)(2,1)S(1)}, bf16[72,1024]{1,0:T(8,128)(2,1...) while((s32[]{:T(128)}, bf16[2,72,512]{2,1,0:T(8,128)(2,1)S(1)}, ...), condition=%wide.region_4.4_spmd, body=%wide.region_1.3_spmd.sunk | while | flops 155749376 | bytes 6744219 | solution.py:40
  86.0 8.6 %while.22 = (s32[]{:T(128)}, bf16[2,72,512]{2,1,0:T(8,128)(2,1)S(1)}, s32[2]{0:T(128)S(1)}, bf16[72,1024]{1,0:T(8,128)(2,1)S(1)}, bf16[72,1024]{1,0:T(8,128)(2,1...) while((s32[]{:T(128)}, bf16[2,72,512]{2,1,0:T(8,128)(2,1)S(1)}, ...), condition=%wide.region_4.4_spmd, body=%wide.region_1.3_spmd.sunk | while | flops 155749376 | bytes 6744219 | solution.py:40
  97.9 4.4 %all-to-all-start.3 = ((bf16[1,4,72,1024]{2,1,0,3:T(4,128)(2,1)}), bf16[1,4,72,1024]{2,1,0,3:T(4,128)(2,1)}, u32[]{:S(2)}, u32[]{:S(2)}) async-start(bf16[1,4,72,1024]{2,1,0,3:T(4,128)(2,1)} %bitcast.123), calls=%async_computation.3 | async-start | bytes 2097152 | tf_op jit(solution)/shard_map/all_to_all | solution.py:80
  102.5 11.4 %all-to-all-done.3 = bf16[1,4,72,1024]{2,1,0,3:T(4,128)(2,1)} async-done(((bf16[1,4,72,1024]{2,1,0,3:T(4,128)(2,1)}), bf16[1,4,72,1024]{2,1,0,3:T(4,128)(2,1)}, u32[]{:S(2)}, u32[]{:S(2)}) %all-to-all-start.3) | async-done | bytes 589856 | tf_op jit(solution)/shard_map/all_to_all | solution.py:80
  115.4 3.0 fusion.44
  119.7 3.7 gather_fusion
  125.3 46.8 %all_to_all.87 = bf16[8,96,1152]{2,1,0:T(8,128)(2,1)} all-to-all(bf16[8,96,1152]{2,1,0:T(8,128)(2,1)S(1)} %select_select_fusion), channel_id=1, replica_groups=mesh['frame'=8,'tok'=4] {'frame'}, dimensions={0} | all-to-all | bytes 3538944 | tf_op jit(solution)/shard_map/all_to_all | solution.py:98
  172.8 61.5 %all-reduce.2.cloned.1.call-done = bf16[768,1152]{1,0:T(8,128)(2,1)} async-done(((bf16[768,1152]{1,0:T(8,128)(2,1)}), bf16[768,1152]{1,0:T(8,128)(2,1)}) %all-reduce.2.cloned.1.call-update) | async-done | bytes 1769488 | tf_op jit(solution)/shard_map/psum | solution.py:99
  234.2 8.8 %fusion.15 = bf16[1,768,1152]{2,1,0:T(8,128)(2,1)} fusion(bf16[1,1152,1152]{2,1,0:T(8,128)(2,1)S(1)} %copy-done, bf16[768,1152]{1,0:T(8,128)(2,1)} %all-reduce.2.cloned.1.call-done, bf16[1,1152,1152]{2,1,0:T(8,128)(2,1)} %param.26, f32[1152]{0:T(1024)S(1)} %reduce.5), kind=kOutput, calls=%fused_computation.29 | convolution fusion | flops 4086595584 | bytes 8851968 | tf_op jit(solution)/shard_map/erf,efd->erd/dot_general | solution.py:105
  243.0 8.8 %copy.95 = bf16[1,768,1152]{1,0,2:T(2,128)(2,1)} copy(bf16[1,768,1152]{2,1,0:T(8,128)(2,1)} %fusion.15) | data formatting | bytes 3538944
  251.9 3.5 copy.103
  256.2 31.8 %reduce-scatter.4.cloned.1.call-done = bf16[288,768]{1,0:T(8,128)(2,1)} async-done(((bf16[1152,768]{1,0:T(8,128)(2,1)}), bf16[288,768]{1,0:T(8,128)(2,1)}) %reduce-scatter.4.cloned.1.call-update) | async-done | bytes 442384
  290.4 4.6 %copy.90 = bf16[1,768,288]{2,0,1:T(2,128)(2,1)} copy(bf16[1,768,288]{1,2,0:T(8,128)(2,1)} %add_convert_fusion.1) | data formatting | bytes 884736 | tf_op jit(solution)/shard_map/convert_element_type | solution.py:115
  295.5 6.1 %reduce.13 = bf16[768,288]{1,0:T(8,128)(2,1)} reduce(bf16[768,1,288]{2,1,0:T(2,128)(2,1)} %bitcast.121, bf16[]{:T(256)} %broadcast.265), dimensions={1}, to_apply=%bitcast.92.reduce_sub_computation | reduce | bytes 884738
  301.6 2.6 reshape.249
  304.3 18.3 %all_to_all.88 = bf16[8,2,13824]{2,1,0:T(2,128)(2,1)} all-to-all(bf16[8,2,13824]{2,1,0:T(2,128)(2,1)} %reshape.249), channel_id=1, replica_groups=mesh['frame'=8,'tok'=4] {'frame'}, dimensions={0} | all-to-all | bytes 884736 | tf_op jit(solution)/shard_map/all_to_all | solution.py:116
  322.5 3.8 reshape.250
  326.3 4.5 %copy.91 = bf16[1,768,288]{1,2,0:T(8,128)(2,1)} copy(bf16[1,768,288]{2,0,1:T(2,128)(2,1)} %bitcast.122) | data formatting | bytes 884736 | tf_op jit(solution)/shard_map/all_to_all | solution.py:116
  330.8 2.5 all_to_all.80
  334.0 6.5 %gather_fusion.1 = bf16[768]{0:T(1024)(128)(2,1)S(1)} fusion(bf16[8,256]{1,0:T(8,128)(2,1)S(1)} %fusion.28, s32[768]{0:T(1024)S(1)} %reshape.231), kind=kCustom, calls=%fused_computation.1 | custom fusion | bytes 9216 | tf_op jit(solution)/shard_map/jit(take_along_axis)/gather | solution.py:118
  340.5 28.3 %all-gather.2.cloned.1.call-done = bf16[8,96,1152]{1,0,2:T(8,128)(2,1)} async-done(((bf16[8,96,288]{1,0,2:T(8,128)(2,1)}), bf16[8,96,1152]{1,0,2:T(8,128)(2,1)}) %all-gather.2.cloned.1.call-update) | async-done | bytes 1769488 | tf_op jit(solution)/shard_map/all_gather | solution.py:117
  368.8 4.2 %copy.92 = bf16[8,96,1152]{2,1,0:T(8,128)(2,1)} copy(bf16[8,96,1152]{1,0,2:T(8,128)(2,1)} %all-gather.2.cloned.1.call-done) | data formatting | bytes 3538944 | tf_op jit(solution)/shard_map/all_gather | solution.py:117
  373.0 3.3 fusion.24
  (119 shorter events, 57.8 us)
Async XLA Ops:
  6.5 227.7 %copy-start = (bf16[1,1152,1152]{2,1,0:T(8,128)(2,1)S(1)}, bf16[1,1152,1152]{2,1,0:T(8,128)(2,1)}, u32[]{:S(2)}) copy-start(bf16[1,1152,1152]{2,1,0:T(8,128)(2,1)} %param.28) | copy-start | bytes 7962628
  8.8 13.9 %all-to-all-start = ((bf16[4,4,72,256]{3,2,1,0:T(8,128)(2,1)}), bf16[4,4,72,256]{3,2,1,0:T(8,128)(2,1)S(1)}, u32[]{:S(2)}, u32[]{:S(2)}) async-start(bf16[4,4,72,256]{3,2,1,0:T(8,128)(2,1)} %bitcast.128), calls=%async_computation | async-start | bytes 1179648 | tf_op jit(solution)/shard_map/all_to_all | solution.py:75
  14.0 15.2 %copy-start.5 = (s32[8,1,96]{2,1,0:T(1,128)S(1)}, s32[8,1,96]{2,1,0:T(1,128)}, u32[]{:S(2)}) copy-start(s32[8,1,96]{2,1,0:T(1,128)} %param.31) | copy-start | bytes 9220
  22.7 16.7 %copy-start.3 = (f32[1,4,1152]{2,1,0:T(4,128)S(1)}, f32[1,4,1152]{2,1,0:T(4,128)}, u32[]{:S(2)}) copy-start(f32[1,4,1152]{2,1,0:T(4,128)} %param.22) | copy-start | bytes 55300
  22.7 12.4 %all-to-all-start.1 = ((bf16[4,4,72,256]{3,2,1,0:T(8,128)(2,1)}), bf16[4,4,72,256]{3,2,1,0:T(8,128)(2,1)}, u32[]{:S(2)}, u32[]{:S(2)}) async-start(bf16[4,4,72,256]{3,2,1,0:T(8,128)(2,1)} %bitcast.127), calls=%async_computation.1 | async-start | bytes 1179648 | tf_op jit(solution)/shard_map/all_to_all | solution.py:76
  35.1 11.7 %all-to-all-start.2 = ((bf16[4,4,72,256]{3,2,1,0:T(8,128)(2,1)}), bf16[4,4,72,256]{3,2,1,0:T(8,128)(2,1)}, u32[]{:S(2)}, u32[]{:S(2)}) async-start(bf16[4,4,72,256]{3,2,1,0:T(8,128)(2,1)} %bitcast.126), calls=%async_computation.2 | async-start | bytes 1179648 | tf_op jit(solution)/shard_map/all_to_all | solution.py:77
  95.6 6.8 %copy-start.6 = (s32[8,1]{0,1:T(1,128)S(1)}, s32[8,1]{0,1:T(1,128)}, u32[]{:S(2)}) copy-start(s32[8,1]{0,1:T(1,128)} %param.30) | copy-start | bytes 100
  97.9 17.4 %copy-start.7 = (f32[1152]{0:T(1024)S(1)}, f32[1152]{0:T(1024)}, u32[]{:S(2)}) copy-start(f32[1152]{0:T(1024)} %param.24) | copy-start | bytes 13828
  97.9 15.9 %all-to-all-start.3 = ((bf16[1,4,72,1024]{2,1,0,3:T(4,128)(2,1)}), bf16[1,4,72,1024]{2,1,0,3:T(4,128)(2,1)}, u32[]{:S(2)}, u32[]{:S(2)}) async-start(bf16[1,4,72,1024]{2,1,0,3:T(4,128)(2,1)} %bitcast.123), calls=%async_computation.3 | async-start | bytes 2097152 | tf_op jit(solution)/shard_map/all_to_all | solution.py:80
  102.3 131.9 %all-reduce.2.cloned.1.call-start = ((), (), s32[]{:S(2)}) async-start(), calls=%async_computation.7 | async-start | bytes 3538944 | tf_op jit(solution)/shard_map/psum | solution.py:99
  118.4 1.0 copy-start.1
  172.0 0.7 copy-start.4
  172.1 116.0 %reduce-scatter.4.cloned.1.call-start = ((), (), s32[]{:S(2)}) async-start(), calls=%async_computation.9 | async-start | bytes 2211840
  255.4 113.4 %all-gather.2.cloned.1.call-start = ((), (), s32[]{:S(2)}) async-start(), calls=%async_computation.8 | async-start | bytes 2949120 | tf_op jit(solution)/shard_map/all_gather | solution.py:117
  326.3 7.4 %copy-start.2 = (bf16[1152,8]{0,1:T(8,128)(2,1)S(1)}, bf16[1152,8]{0,1:T(8,128)(2,1)}, u32[]{:S(2)}) copy-start(bf16[1152,8]{0,1:T(8,128)(2,1)} %param.25) | copy-start | bytes 55300
Sparse Core Ops, SparseCore 0:
  172.2 61.9 all-reduce.1
  255.5 32.4 reduce-scatter.3
  333.4 35.2 all-gather.1
where the time goes:
time: 385 us; the launch traced here: 383 us
  waiting for transfers between devices  147 us (38%)
  local copies, waits for them, and re-layouts  84.9 us (22%)
  blocking collectives  65.1 us (17%)
  matrix products  25.9 us (7%)
  starting transfers between devices  18.3 us (5%)
  loops' own time  14.9 us (4%)
  other arithmetic  13.9 us (4%)
  between operations  13.3 us (3%)
    psum x1, waiting for transfers between devices, per_device(): lax.psum(moved.astype(jnp.float32).astype(jnp.bfloat16), 'tok')  61.5 us
    all_to_all x1, blocking collectives, per_device(): lax.all_to_all(chosen, 'frame', split_axis=0, concat_axis=1, tiled=True)  46.8 us
    unnamed x4, waiting for transfers between devices  31.9 us
    unnamed x25, local copies, waits for them, and re-layouts  28.5 us
    all_gather x1, waiting for transfers between devices, per_device(): returned_rows = lax.all_gather(returned_cols, 'tok', axis=2, tiled=True)  28.3 us
    all_to_all x1, blocking collectives, per_device(): lax.all_to_all(expert_out, 'frame', split_axis=1, concat_axis=0, tiled=True)  18.3 us
    another operation x4, loops' own time, head_attention(): blocks = lax.map(one_block, starts)  14.8 us
    all_to_all x1, waiting for transfers between devices, per_device(): lax.all_to_all(attended, 'tok', split_axis=3, concat_axis=0, tiled=True)  11.4 us
  transfers between devices with their start and end apart: 7, of which 7 were waited for; matrix products, arithmetic and copies ran while one was open for 5% of the time, Pallas kernels for 0%

commit v1 on v0

--- a/solution.py
+++ b/solution.py
@@ -3,6 +3,7 @@
 import jax.numpy as jnp
 from jax import lax
 from jax.sharding import PartitionSpec as P
+from jax.lax import all_gather
 
 H = 16
 HD = 72
@@ -114,7 +115,7 @@
     )
     expert_out = (summed + bias_part[:, None, :]).astype(jnp.bfloat16)
     returned_cols = lax.all_to_all(expert_out, "frame", split_axis=1, concat_axis=0, tiled=True)
-    returned_rows = lax.all_gather(returned_cols, "tok", axis=2, tiled=True)
+    returned_rows = jnp.concatenate(all_gather(returned_cols, axis_name="tok"), axis=2)
     mix_weight = jnp.take_along_axis(gate_values.T, safe_pos, axis=1)
     mix_weight = jnp.where(on_shard, mix_weight, jnp.zeros_like(mix_weight)).astype(jnp.bfloat16)
     targets = jnp.arange(tok_local, dtype=jnp.int32)

time: 385 us -> 385 us (level)
    all_to_all x2 -> x0, local copies, waits for them, and re-layouts: 6.99 us -> none  [per_device(): lax.all_to_all(expert_out, 'frame', split_axis=1, concat_axis=0, tiled=True)]
    another operation x0 -> x1, local copies, waits for them, and re-layouts: none -> 4.69 us  [per_device(): returned_rows.reshape(-1, model_width)]
    reshape x0 -> x1, local copies, waits for them, and re-layouts: none -> 4.53 us  [per_device(): jnp.concatenate(all_gather(returned_cols, axis_name='tok'), axis=2)]
    all_gather x1 -> x0, local copies, waits for them, and re-layouts: 4.22 us -> none  [per_device(): returned_rows = lax.all_gather(returned_cols, 'tok', axis=2, tiled=True)]
    unnamed x25 -> x26, local copies, waits for them, and re-layouts: 28.5 us -> 30.7 us
where the time goes in v1:
time: 385 us; the launch traced here: 383 us
  waiting for transfers between devices  147 us (38%)
  local copies, waits for them, and re-layouts  85 us (22%)
  blocking collectives  65.1 us (17%)
  matrix products  26 us (7%)
  starting transfers between devices  18.3 us (5%)
  loops' own time  14.9 us (4%)
  other arithmetic  13.9 us (4%)
  between operations  13.3 us (3%)
    psum x1, waiting for transfers between devices, per_device(): lax.psum(moved.astype(jnp.float32).astype(jnp.bfloat16), 'tok')  61.5 us
    all_to_all x1, blocking collectives, per_device(): lax.all_to_all(chosen, 'frame', split_axis=0, concat_axis=1, tiled=True)  46.8 us
    unnamed x4, waiting for transfers between devices  31.9 us
    unnamed x26, local copies, waits for them, and re-layouts  30.7 us
    all_gather x1, waiting for transfers between devices, per_device(): all_gather(returned_cols, axis_name='tok')  28.3 us
    all_to_all x1, blocking collectives, per_device(): lax.all_to_all(expert_out, 'frame', split_axis=1, concat_axis=0, tiled=True)  18.3 us
    another operation x4, loops' own time, head_attention(): blocks = lax.map(one_block, starts)  14.8 us
    all_to_all x1, waiting for transfers between devices, per_device(): lax.all_to_all(attended, 'tok', split_axis=3, concat_axis=0, tiled=True)  11.4 us
  transfers between devices with their start and end apart: 7, of which 7 were waited for; matrix products, arithmetic and copies ran while one was open for 5% of the time, Pallas kernels for 0%

profile of v1, /device:TPU:0, one launch (start us, length us, event | category | flops | bytes accessed | tf_op | source)
XLA Modules:
  0.0 383.1 jit_solution(17712531784272706513)
XLA Ops:
  8.8 5.2 %all-to-all-start = ((bf16[4,4,72,256]{3,2,1,0:T(8,128)(2,1)}), bf16[4,4,72,256]{3,2,1,0:T(8,128)(2,1)S(1)}, u32[]{:S(2)}, u32[]{:S(2)}) async-start(bf16[4,4,72,256]{3,2,1,0:T(8,128)(2,1)} %bitcast.133), calls=%async_computation | async-start | bytes 1179648 | tf_op jit(solution)/shard_map/all_to_all | solution.py:76
  16.1 6.6 %all-to-all-done = bf16[4,4,72,256]{3,2,1,0:T(8,128)(2,1)S(1)} async-done(((bf16[4,4,72,256]{3,2,1,0:T(8,128)(2,1)}), bf16[4,4,72,256]{3,2,1,0:T(8,128)(2,1)S(1)}, u32[]{:S(2)}, u32[]{:S(2)}) %all-to-all-start) | async-done | bytes 589856 | tf_op jit(solution)/shard_map/all_to_all | solution.py:76
  22.7 4.3 %all-to-all-start.1 = ((bf16[4,4,72,256]{3,2,1,0:T(8,128)(2,1)}), bf16[4,4,72,256]{3,2,1,0:T(8,128)(2,1)}, u32[]{:S(2)}, u32[]{:S(2)}) async-start(bf16[4,4,72,256]{3,2,1,0:T(8,128)(2,1)} %bitcast.132), calls=%async_computation.1 | async-start | bytes 1179648 | tf_op jit(solution)/shard_map/all_to_all | solution.py:77
  29.2 5.9 %all-to-all-done.1 = bf16[4,4,72,256]{3,2,1,0:T(8,128)(2,1)} async-done(((bf16[4,4,72,256]{3,2,1,0:T(8,128)(2,1)}), bf16[4,4,72,256]{3,2,1,0:T(8,128)(2,1)}, u32[]{:S(2)}, u32[]{:S(2)}) %all-to-all-start.1) | async-done | bytes 589856 | tf_op jit(solution)/shard_map/all_to_all | solution.py:77
  35.1 4.2 %all-to-all-start.2 = ((bf16[4,4,72,256]{3,2,1,0:T(8,128)(2,1)}), bf16[4,4,72,256]{3,2,1,0:T(8,128)(2,1)}, u32[]{:S(2)}, u32[]{:S(2)}) async-start(bf16[4,4,72,256]{3,2,1,0:T(8,128)(2,1)} %bitcast.131), calls=%async_computation.2 | async-start | bytes 1179648 | tf_op jit(solution)/shard_map/all_to_all | solution.py:78
  40.8 2.4 squeeze.27
  49.6 45.9 %while.21 = (s32[]{:T(128)}, bf16[4,72,1024]{2,1,0:T(8,128)(2,1)}, bf16[4,72,1024]{2,1,0:T(8,128)(2,1)}, bf16[4,72,1024]{2,1,0:T(8,128)(2,1)}, bf16[4,72,1024]{2...) while((s32[]{:T(128)}, bf16[4,72,1024]{2,1,0:T(8,128)(2,1)}, ...), condition=%wide.region_5.6_spmd, body=%wide.region_0.5_spmd.sunk | while | flops 155749376 | bytes 8513900 | solution.py:46
  51.6 8.6 %while.22 = (s32[]{:T(128)}, bf16[2,72,512]{2,1,0:T(8,128)(2,1)S(1)}, s32[2]{0:T(128)S(1)}, bf16[72,1024]{1,0:T(8,128)(2,1)S(1)}, bf16[72,1024]{1,0:T(8,128)(2,1...) while((s32[]{:T(128)}, bf16[2,72,512]{2,1,0:T(8,128)(2,1)S(1)}, ...), condition=%wide.region_4.4_spmd, body=%wide.region_1.3_spmd.sunk | while | flops 155749376 | bytes 6744219 | solution.py:41
  63.1 8.6 %while.22 = (s32[]{:T(128)}, bf16[2,72,512]{2,1,0:T(8,128)(2,1)S(1)}, s32[2]{0:T(128)S(1)}, bf16[72,1024]{1,0:T(8,128)(2,1)S(1)}, bf16[72,1024]{1,0:T(8,128)(2,1...) while((s32[]{:T(128)}, bf16[2,72,512]{2,1,0:T(8,128)(2,1)S(1)}, ...), condition=%wide.region_4.4_spmd, body=%wide.region_1.3_spmd.sunk | while | flops 155749376 | bytes 6744219 | solution.py:41
  74.6 8.6 %while.22 = (s32[]{:T(128)}, bf16[2,72,512]{2,1,0:T(8,128)(2,1)S(1)}, s32[2]{0:T(128)S(1)}, bf16[72,1024]{1,0:T(8,128)(2,1)S(1)}, bf16[72,1024]{1,0:T(8,128)(2,1...) while((s32[]{:T(128)}, bf16[2,72,512]{2,1,0:T(8,128)(2,1)S(1)}, ...), condition=%wide.region_4.4_spmd, body=%wide.region_1.3_spmd.sunk | while | flops 155749376 | bytes 6744219 | solution.py:41
  86.0 8.6 %while.22 = (s32[]{:T(128)}, bf16[2,72,512]{2,1,0:T(8,128)(2,1)S(1)}, s32[2]{0:T(128)S(1)}, bf16[72,1024]{1,0:T(8,128)(2,1)S(1)}, bf16[72,1024]{1,0:T(8,128)(2,1...) while((s32[]{:T(128)}, bf16[2,72,512]{2,1,0:T(8,128)(2,1)S(1)}, ...), condition=%wide.region_4.4_spmd, body=%wide.region_1.3_spmd.sunk | while | flops 155749376 | bytes 6744219 | solution.py:41
  95.6 2.3 copy.88
  97.9 4.4 %all-to-all-start.3 = ((bf16[1,4,72,1024]{2,1,0,3:T(4,128)(2,1)}), bf16[1,4,72,1024]{2,1,0,3:T(4,128)(2,1)}, u32[]{:S(2)}, u32[]{:S(2)}) async-start(bf16[1,4,72,1024]{2,1,0,3:T(4,128)(2,1)} %bitcast.126), calls=%async_computation.3 | async-start | bytes 2097152 | tf_op jit(solution)/shard_map/all_to_all | solution.py:81
  102.5 11.4 %all-to-all-done.3 = bf16[1,4,72,1024]{2,1,0,3:T(4,128)(2,1)} async-done(((bf16[1,4,72,1024]{2,1,0,3:T(4,128)(2,1)}), bf16[1,4,72,1024]{2,1,0,3:T(4,128)(2,1)}, u32[]{:S(2)}, u32[]{:S(2)}) %all-to-all-start.3) | async-done | bytes 589856 | tf_op jit(solution)/shard_map/all_to_all | solution.py:81
  115.4 3.0 fusion.44
  119.7 3.7 gather_fusion
  125.3 46.8 %all_to_all.87 = bf16[8,96,1152]{2,1,0:T(8,128)(2,1)} all-to-all(bf16[8,96,1152]{2,1,0:T(8,128)(2,1)S(1)} %select_select_fusion), channel_id=1, replica_groups=mesh['frame'=8,'tok'=4] {'frame'}, dimensions={0} | all-to-all | bytes 3538944 | tf_op jit(solution)/shard_map/all_to_all | solution.py:99
  172.8 61.5 %all-reduce.2.cloned.1.call-done = bf16[768,1152]{1,0:T(8,128)(2,1)} async-done(((bf16[768,1152]{1,0:T(8,128)(2,1)}), bf16[768,1152]{1,0:T(8,128)(2,1)}) %all-reduce.2.cloned.1.call-update) | async-done | bytes 1769488 | tf_op jit(solution)/shard_map/psum | solution.py:100
  234.2 8.8 %fusion.15 = bf16[1,768,1152]{2,1,0:T(8,128)(2,1)} fusion(bf16[1,1152,1152]{2,1,0:T(8,128)(2,1)S(1)} %copy-done, bf16[768,1152]{1,0:T(8,128)(2,1)} %all-reduce.2.cloned.1.call-done, bf16[1,1152,1152]{2,1,0:T(8,128)(2,1)} %param.26, f32[1152]{0:T(1024)S(1)} %reduce.5), kind=kOutput, calls=%fused_computation.29 | convolution fusion | flops 4086595584 | bytes 8851968 | tf_op jit(solution)/shard_map/erf,efd->erd/dot_general | solution.py:106
  243.0 8.8 %copy.101 = bf16[1,768,1152]{1,0,2:T(2,128)(2,1)} copy(bf16[1,768,1152]{2,1,0:T(8,128)(2,1)} %fusion.15) | data formatting | bytes 3538944
  251.9 3.5 copy.110
  256.2 31.8 %reduce-scatter.4.cloned.1.call-done = bf16[288,768]{1,0:T(8,128)(2,1)} async-done(((bf16[1152,768]{1,0:T(8,128)(2,1)}), bf16[288,768]{1,0:T(8,128)(2,1)}) %reduce-scatter.4.cloned.1.call-update) | async-done | bytes 442384
  290.4 4.6 %copy.94 = bf16[1,768,288]{2,0,1:T(2,128)(2,1)} copy(bf16[1,768,288]{1,2,0:T(8,128)(2,1)} %add_convert_fusion.1) | data formatting | bytes 884736 | tf_op jit(solution)/shard_map/convert_element_type | solution.py:116
  295.5 6.1 %reduce.13 = bf16[768,288]{1,0:T(8,128)(2,1)} reduce(bf16[768,1,288]{2,1,0:T(2,128)(2,1)} %bitcast.124, bf16[]{:T(256)} %broadcast.265), dimensions={1}, to_apply=%bitcast.95.reduce_sub_computation | reduce | bytes 884738
  301.6 2.6 reshape.250
  304.3 18.3 %all_to_all.88 = bf16[8,2,13824]{2,1,0:T(2,128)(2,1)} all-to-all(bf16[8,2,13824]{2,1,0:T(2,128)(2,1)} %reshape.250), channel_id=1, replica_groups=mesh['frame'=8,'tok'=4] {'frame'}, dimensions={0} | all-to-all | bytes 884736 | tf_op jit(solution)/shard_map/all_to_all | solution.py:117
  322.5 3.8 reshape.251
  329.2 6.5 %gather_fusion.1 = bf16[768]{0:T(1024)(128)(2,1)S(1)} fusion(bf16[8,256]{1,0:T(8,128)(2,1)S(1)} %fusion.28, s32[768]{0:T(1024)S(1)} %reshape.231), kind=kCustom, calls=%fused_computation.1 | custom fusion | bytes 9216 | tf_op jit(solution)/shard_map/jit(take_along_axis)/gather | solution.py:119
  335.7 28.3 %all-gather.2.cloned.1.call-done = bf16[4,8,96,288]{3,2,1,0:T(8,128)(2,1)} async-done(((bf16[1,8,96,288]{3,2,1,0:T(8,128)(2,1)}), bf16[4,8,96,288]{3,2,1,0:T(8,128)(2,1)}) %all-gather.2.cloned.1.call-update) | async-done | bytes 1769488 | tf_op jit(solution)/shard_map/all_gather | solution.py:118
  364.0 4.5 %copy.97 = bf16[8,96,4,288]{1,0,3,2:T(8,128)(2,1)} copy(bf16[8,96,4,288]{3,1,0,2:T(8,128)(2,1)} %bitcast.129) | data formatting | bytes 3538944 | tf_op jit(solution)/shard_map/reshape | solution.py:118
  368.5 4.7 %reshape_reshape.3 = bf16[768,1152]{0,1:T(8,128)(2,1)} reshape(bf16[8,96,4,288]{1,0,3,2:T(8,128)(2,1)} %copy.97) | data formatting | bytes 3538944 | tf_op jit(solution)/shard_map/reshape;reshape | solution.py:125
  373.2 3.4 fusion.24
  (119 shorter events, 57.6 us)
Async XLA Ops:
  6.5 227.7 %copy-start = (bf16[1,1152,1152]{2,1,0:T(8,128)(2,1)S(1)}, bf16[1,1152,1152]{2,1,0:T(8,128)(2,1)}, u32[]{:S(2)}) copy-start(bf16[1,1152,1152]{2,1,0:T(8,128)(2,1)} %param.28) | copy-start | bytes 7962628
  8.8 13.9 %all-to-all-start = ((bf16[4,4,72,256]{3,2,1,0:T(8,128)(2,1)}), bf16[4,4,72,256]{3,2,1,0:T(8,128)(2,1)S(1)}, u32[]{:S(2)}, u32[]{:S(2)}) async-start(bf16[4,4,72,256]{3,2,1,0:T(8,128)(2,1)} %bitcast.133), calls=%async_computation | async-start | bytes 1179648 | tf_op jit(solution)/shard_map/all_to_all | solution.py:76
  14.0 15.2 %copy-start.5 = (s32[8,1,96]{2,1,0:T(1,128)S(1)}, s32[8,1,96]{2,1,0:T(1,128)}, u32[]{:S(2)}) copy-start(s32[8,1,96]{2,1,0:T(1,128)} %param.31) | copy-start | bytes 9220
  22.7 16.7 %copy-start.3 = (f32[1,4,1152]{2,1,0:T(4,128)S(1)}, f32[1,4,1152]{2,1,0:T(4,128)}, u32[]{:S(2)}) copy-start(f32[1,4,1152]{2,1,0:T(4,128)} %param.22) | copy-start | bytes 55300
  22.7 12.4 %all-to-all-start.1 = ((bf16[4,4,72,256]{3,2,1,0:T(8,128)(2,1)}), bf16[4,4,72,256]{3,2,1,0:T(8,128)(2,1)}, u32[]{:S(2)}, u32[]{:S(2)}) async-start(bf16[4,4,72,256]{3,2,1,0:T(8,128)(2,1)} %bitcast.132), calls=%async_computation.1 | async-start | bytes 1179648 | tf_op jit(solution)/shard_map/all_to_all | solution.py:77
  35.1 11.7 %all-to-all-start.2 = ((bf16[4,4,72,256]{3,2,1,0:T(8,128)(2,1)}), bf16[4,4,72,256]{3,2,1,0:T(8,128)(2,1)}, u32[]{:S(2)}, u32[]{:S(2)}) async-start(bf16[4,4,72,256]{3,2,1,0:T(8,128)(2,1)} %bitcast.131), calls=%async_computation.2 | async-start | bytes 1179648 | tf_op jit(solution)/shard_map/all_to_all | solution.py:78
  95.6 6.8 %copy-start.6 = (s32[8,1]{0,1:T(1,128)S(1)}, s32[8,1]{0,1:T(1,128)}, u32[]{:S(2)}) copy-start(s32[8,1]{0,1:T(1,128)} %param.30) | copy-start | bytes 100
  97.9 17.4 %copy-start.7 = (f32[1152]{0:T(1024)S(1)}, f32[1152]{0:T(1024)}, u32[]{:S(2)}) copy-start(f32[1152]{0:T(1024)} %param.24) | copy-start | bytes 13828
  97.9 15.9 %all-to-all-start.3 = ((bf16[1,4,72,1024]{2,1,0,3:T(4,128)(2,1)}), bf16[1,4,72,1024]{2,1,0,3:T(4,128)(2,1)}, u32[]{:S(2)}, u32[]{:S(2)}) async-start(bf16[1,4,72,1024]{2,1,0,3:T(4,128)(2,1)} %bitcast.126), calls=%async_computation.3 | async-start | bytes 2097152 | tf_op jit(solution)/shard_map/all_to_all | solution.py:81
  102.3 131.9 %all-reduce.2.cloned.1.call-start = ((), (), s32[]{:S(2)}) async-start(), calls=%async_computation.7 | async-start | bytes 3538944 | tf_op jit(solution)/shard_map/psum | solution.py:100
  118.4 1.0 copy-start.1
  172.0 0.7 copy-start.4
  172.1 116.0 %reduce-scatter.4.cloned.1.call-start = ((), (), s32[]{:S(2)}) async-start(), calls=%async_computation.9 | async-start | bytes 2211840
  255.4 108.6 %all-gather.2.cloned.1.call-start = ((), (), s32[]{:S(2)}) async-start(), calls=%async_computation.8 | async-start | bytes 2949120 | tf_op jit(solution)/shard_map/all_gather | solution.py:118
  322.5 6.4 %copy-start.2 = (bf16[1152,8]{0,1:T(8,128)(2,1)S(1)}, bf16[1152,8]{0,1:T(8,128)(2,1)}, u32[]{:S(2)}) copy-start(bf16[1152,8]{0,1:T(8,128)(2,1)} %param.25) | copy-start | bytes 55300
Sparse Core Ops, SparseCore 0:
  172.2 61.9 all-reduce.1
  255.5 32.4 reduce-scatter.3
  328.6 35.2 all-gather.1
